TPU v7x, 32 devices: a whole 2x2x4 slice. The times are simulated.
32 devices in a mesh: scene: 4 (over x, core), view: 4 (over z), half: 2 (over y).
Axes of the slice: x: 2, y: 2, z: 4, core: 2. Of those that a mesh axis runs over, the one named last changes fastest.
Arguments:
- tokens: bfloat16 [16, 512, 2048], P(('scene', 'view'), 'half'), parts along dimension 0, may hold values from -9 to 12
- w_qkv: bfloat16 [2048, 768], replicated, may hold values from -0.125 to 0.125
- w_out: bfloat16 [256, 2048], replicated, may hold values from -5 to 5
- key_lists: int32 [16, 4, 2], P(('scene', 'view'), 'half'), parts along dimension 0, may hold values from 0 to 15, as said below
- list_len: int32 [16, 4], P(('scene', 'view'), 'half'), parts along dimension 0, may hold values from 1 to 2, as said below
Outputs:
- mixed: bfloat16 [16, 512, 2048], P(('scene', 'view'), 'half'), parts along dimension 0
There are 4 independent parts, one for each index of `scene`. A program takes and returns all parts, laid end to end along the dimension named above; an argument that names none is the same for every part. Nothing has to cross between parts.
Inputs may be any that keep to these rules, and one draw needn't show every extreme that they name: `key_lists`: entries of one list are distinct block ids of the scene. `list_len`: some query block lists 2 blocks in every scene.
All inputs are finite; a program needn't handle non-finite values.
Results may differ from a plain program's by a relative error of at most 0.014.
The roundings to bfloat16 on the way count: a program that leaves them out, or rounds other values in their place, can miss the bound.
Values may be sent and summed in bfloat16 or wider, within the bound.
A program may use at most 64 MiB of HBM per device.

v0:
```python
import jax
import jax.numpy as jnp
from jax import lax
from jax.sharding import PartitionSpec as P

HEADS = 4


NEG = -1e30


def block_mask(lists, lengths, count, block):
    key_rows = jnp.arange(count, dtype=jnp.int32)
    key_block = key_rows // block
    slots = jnp.arange(lists.shape[1], dtype=jnp.int32)
    live = slots[None, :] < lengths[:, None]
    hits = (lists[:, :, None] == key_block[None, None, :]) & live[:, :, None]
    return jnp.any(hits, axis=1)


def attend(state, queries, keys, values, allowed):
    peak, total, accum = state
    heads = accum.shape[1]
    q3 = queries.reshape(queries.shape[0], heads, -1)
    k3 = keys.reshape(keys.shape[0], heads, -1)
    v3 = values.reshape(values.shape[0], heads, -1)
    scores = jnp.einsum("qhd,khd->hqk", q3, k3, preferred_element_type=jnp.float32) * q3.shape[
        2
    ] ** (-0.5)
    masked = jnp.where(allowed[None], scores, NEG)
    fresh = jnp.maximum(peak, jnp.max(masked, axis=2))
    weights = jnp.where(allowed[None], jnp.exp(scores - fresh[:, :, None]), 0.0)
    factor = jnp.exp(peak - fresh)
    total = jnp.sum(weights, axis=2)
    summed = jnp.einsum(
        "hqk,khd->qhd", weights.astype(jnp.bfloat16), v3, preferred_element_type=jnp.float32
    )
    accum = accum * factor.T[:, :, None] + summed
    return (fresh, total, accum)


def visit(state, queries, keys, values, allowed):
    return lax.cond(
        jnp.any(allowed),
        lambda held: attend(held, queries, keys, values, allowed),
        lambda held: held,
        state,
    )


def per_device(tokens, w_qkv, w_out, key_lists, list_len):
    rows = tokens.shape[1]
    width = tokens.shape[2]
    flat = tokens.reshape(rows, width)
    inner = w_out.shape[0]
    head_size = inner // HEADS
    proj = jnp.dot(flat, w_qkv, preferred_element_type=jnp.float32).astype(jnp.bfloat16)
    queries = proj[:, :inner]
    keys = proj[:, inner : 2 * inner]
    values = proj[:, 2 * inner :]
    lists = key_lists.reshape(-1, key_lists.shape[2])
    lengths = list_len.reshape(-1)
    local_blocks = lists.shape[0]
    block = rows // local_blocks
    peak0 = jnp.full((HEADS, rows), NEG, jnp.float32)
    total0 = jnp.zeros((HEADS, rows), jnp.float32)
    accum0 = jnp.zeros((rows, HEADS, head_size), jnp.float32)
    view_keys, view_values = (
        lax.all_gather(keys, "half", axis=0, tiled=True),
        lax.all_gather(values, "half", axis=0, tiled=True),
    )
    piece = (
        lax.all_gather(view_keys, "view", axis=0, tiled=True),
        lax.all_gather(view_values, "view", axis=0, tiled=True),
    )
    count = piece[0].shape[0]
    allowed = jnp.repeat(block_mask(lists, lengths, count, block), block, axis=0)
    peak, total, accum = visit((peak0, total0, accum0), queries, piece[0], piece[1], allowed)
    attn = (accum / total.T[:, :, None]).reshape(rows, inner).astype(jnp.bfloat16)
    mixed = jnp.dot(attn, w_out, preferred_element_type=jnp.float32).astype(jnp.bfloat16)
    return mixed.reshape(1, rows, width)


def solution(mesh):
    placed = (
        P(("scene", "view"), "half", None),
        P(),
        P(),
        P(("scene", "view"), "half", None),
        P(("scene", "view"), "half"),
    )
    return jax.shard_map(
        per_device,
        mesh=mesh,
        in_specs=placed,
        out_specs=P(("scene", "view"), "half", None),
        check_vma=False,
    )
```

profile of v0, /device:TPU:0, one launch (start us, length us, event | category | flops | bytes accessed | tf_op | source)
XLA Modules:
  0.0 109.8 jit_solution(13672634810469193445)
XLA Ops:
  6.5 0.0 copy-start
  6.5 0.0 all-gather.3.cloned.1.call-start
  6.5 1.9 %copy-done = bf16[2048,768]{1,0:T(8,128)(2,1)S(1)} copy-done((bf16[2048,768]{1,0:T(8,128)(2,1)S(1)}, bf16[2048,768]{1,0:T(8,128)(2,1)}, u32[]{:S(2)}) %copy-start) | copy-done | bytes 3145752
  8.4 2.2 %convolution_convert_fusion.1 = bf16[256,768]{1,0:T(8,128)(2,1)S(1)} fusion(bf16[2048,768]{1,0:T(8,128)(2,1)S(1)} %copy-done, bf16[1,256,2048]{2,1,0:T(8,128)(2,1)} %param.7), kind=kOutput, calls=%fused_computation.14 | convolution fusion | flops 805502976 | bytes 4587520 | tf_op jit(solution)/shard_map/dot_general | solution.py:57
  10.6 0.7 fusion.18
  11.3 7.2 %all_gather.12 = bf16[512,256]{1,0:T(8,128)(2,1)} all-gather(bf16[256,256]{1,0:T(8,128)(2,1)S(1)} %get-tuple-element.35), channel_id=1, replica_groups=mesh['scene'=4,'view'=4,'half'=2] {'half'}, dimensions={0}, use_global_device_ids=true | all-gather | bytes 393216 | tf_op jit(solution)/shard_map/all_gather | solution.py:69
  18.5 0.0 all-gather.3.cloned.1.call-update
  18.6 0.0 all-gather.5.cloned.1.call-start
  18.6 7.2 %all_gather.14 = bf16[512,256]{1,0:T(8,128)(2,1)} all-gather(bf16[256,256]{1,0:T(8,128)(2,1)} %get-tuple-element.34), channel_id=1, replica_groups=mesh['scene'=4,'view'=4,'half'=2] {'half'}, dimensions={0}, use_global_device_ids=true | all-gather | bytes 393216 | tf_op jit(solution)/shard_map/all_gather | solution.py:70
  25.8 0.0 all-gather.5.cloned.1.call-update
  25.9 0.7 iota_compare_fusion
  26.6 0.8 and_reduce_fusion
  27.4 1.2 %broadcast_reduce_fusion = pred[]{:T(512)} fusion(pred[2,2048]{1,0:T(4,128)(4,1)S(1)} %and_reduce_fusion), kind=kLoop, calls=%fused_computation.16 | loop fusion | flops 524287 | bytes 4097 | tf_op jit(solution)/shard_map/reduce_or | solution.py:44
  29.2 19.0 %all-gather.3.cloned.1.call-done = bf16[2048,256]{1,0:T(8,128)(2,1)} async-done(((bf16[512,256]{1,0:T(8,128)(2,1)}), bf16[2048,256]{1,0:T(8,128)(2,1)}) %all-gather.3.cloned.1.call-update) | async-done | bytes 1048592 | tf_op jit(solution)/shard_map/all_gather | solution.py:73
  48.2 28.9 %all-gather.5.cloned.1.call-done = bf16[2048,256]{1,0:T(8,128)(2,1)} async-done(((bf16[512,256]{1,0:T(8,128)(2,1)}), bf16[2048,256]{1,0:T(8,128)(2,1)}) %all-gather.5.cloned.1.call-update) | async-done | bytes 1048592 | tf_op jit(solution)/shard_map/all_gather | solution.py:74
  77.1 1.0 broadcast_in_dim.41
  78.2 22.1 %conditional.1 = (f32[4,256]{1,0:T(4,128)S(1)}, f32[256,4,64]{0,2,1:T(8,128)S(1)}) conditional(s32[]{:T(128)} %convert_element_type.18, () %tuple.13, (pred[2,128,2048]{2,1,0:T(8,128)(4,1)}, bf16[256,768]{1,0:T(8,128)(2,1)S(1)}, bf16[2048,256]{1,0:T(8,128)(2,1)}, bf16[2048,256]{1,0:T(8,128)(2,1)}) %tuple.14), branch_computations={%region_2.3_spmd, %region_3.6_spmd} | conditional | flops 560006144 | bytes 68059184 | solution.py:43
  78.2 2.3 %copy.10 = bf16[2048,256]{0,1:T(8,128)(2,1)} copy(bf16[2048,256]{1,0:T(8,128)(2,1)} %get-tuple-element.28) | data formatting | bytes 2097152 | tf_op jit(solution)/shard_map
  80.4 0.9 copy.9
  81.3 0.9 slice.12
  82.3 6.2 %select_reduce_fusion = (f32[4,256]{1,0:T(4,128)S(1)}, f32[4,256,2048]{2,1,0:T(8,128)}) fusion(pred[256,2048]{1,0:T(8,128)(4,1)} %bitcast, bf16[256,4,64]{0,2,1:T(8,128)(2,1)S(1)} %bitcast.27, bf16[2048,4,64]{0,2,1:T(8,128)(2,1)} %bitcast.25), kind=kOutput, calls=%fused_computation.1 | convolution fusion | flops 274725888 | bytes 10096640 | tf_op jit(solution)/shard_map/cond/branch_1_fun/qhd,khd->hqk/dot_general | solution.py:27
  88.5 2.3 %copy.11 = bf16[2048,256]{0,1:T(8,128)(2,1)} copy(bf16[2048,256]{1,0:T(8,128)(2,1)} %get-tuple-element.29) | data formatting | bytes 2097152 | tf_op jit(solution)/shard_map
  90.8 0.0 copy-start.1
  90.8 5.2 %fusion.8 = f32[256,4,64]{0,2,1:T(8,128)S(1)} fusion(bf16[2048,4,64]{0,2,1:T(8,128)(2,1)} %bitcast.26, f32[4,256,2048]{2,1,0:T(8,128)} %get-tuple-element.33, f32[4,256]{1,0:T(4,128)S(1)} %get-tuple-element.31, pred[256,2048]{1,0:T(8,128)(4,1)} %bitcast, f32[256,4]{0,1:T(4,128)S(1)} %get-tuple-element.30), kind=kOutput, calls=%fused_computation.7 | convolution fusion | flops 276889600 | bytes 10231808 | tf_op jit(solution)/shard_map/cond/branch_1_fun/hqk,khd->qhd/dot_general | solution.py:35
  96.0 1.1 %copy-done.1 = f32[4,256,2048]{2,1,0:T(8,128)S(1)} copy-done((f32[4,256,2048]{2,1,0:T(8,128)S(1)}, f32[4,256,2048]{2,1,0:T(8,128)}, u32[]{:S(2)}) %copy-start.1) | copy-done | bytes 8388632 | tf_op jit(solution)/shard_map/cond
  97.1 3.2 %fusion.1 = f32[4,256]{1,0:T(4,128)S(1)} fusion(f32[4,256,2048]{2,1,0:T(8,128)S(1)} %copy-done.1, f32[4,256]{1,0:T(4,128)S(1)} %get-tuple-element.31, pred[256,2048]{1,0:T(8,128)(4,1)} %bitcast), kind=kLoop, calls=%fused_computation.3 | loop fusion | flops 8387584 | bytes 8921088 | tf_op jit(solution)/shard_map/cond/branch_1_fun/reduce_sum | solution.py:34
  100.3 2.7 %fusion.13 = bf16[1,256,2048]{2,1,0:T(8,128)(2,1)} fusion(bf16[256,256]{0,1:T(8,128)(2,1)S(1)} %bitcast.28, bf16[256,2048]{1,0:T(8,128)(2,1)} %param.9), kind=kOutput, calls=%fused_computation.13 | convolution fusion | flops 268959744 | bytes 2228224 | tf_op jit(solution)/shard_map/dot_general | solution.py:80
  (3 shorter events, 0.0 us)
Async XLA Ops:
  6.5 1.9 %copy-start = (bf16[2048,768]{1,0:T(8,128)(2,1)S(1)}, bf16[2048,768]{1,0:T(8,128)(2,1)}, u32[]{:S(2)}) copy-start(bf16[2048,768]{1,0:T(8,128)(2,1)} %param.8) | copy-start | bytes 9437188
  6.5 41.7 %all-gather.3.cloned.1.call-start = ((), (), s32[]{:S(2)}) async-start(), calls=%async_computation | async-start | bytes 1310720 | tf_op jit(solution)/shard_map/all_gather | solution.py:73
  18.6 58.6 %all-gather.5.cloned.1.call-start = ((), (), s32[]{:S(2)}) async-start(), calls=%async_computation.1 | async-start | bytes 1310720 | tf_op jit(solution)/shard_map/all_gather | solution.py:74
  90.8 6.3 %copy-start.1 = (f32[4,256,2048]{2,1,0:T(8,128)S(1)}, f32[4,256,2048]{2,1,0:T(8,128)}, u32[]{:S(2)}) copy-start(f32[4,256,2048]{2,1,0:T(8,128)} %get-tuple-element.33) | copy-start | bytes 25165828 | tf_op jit(solution)/shard_map/cond
Sparse Core Ops, SparseCore 0:
  18.7 29.4 all-gather.2
  49.8 27.3 all-gather.4
where the time goes:
time: 110 us
  waiting for transfers between devices  47.9 us (44%)
  matrix products  16.3 us (15%)
  blocking collectives  14.4 us (13%)
  between operations  14.1 us (13%)
  local copies, waits for them, and re-layouts  11.1 us (10%)
  other arithmetic  5.97 us (5%)
    all_gather x1, waiting for transfers between devices, per_device(): lax.all_gather(view_values, 'view', axis=0, tiled=True)  28.9 us
    all_gather x1, waiting for transfers between devices, per_device(): lax.all_gather(view_keys, 'view', axis=0, tiled=True)  19 us
    all_gather x1, blocking collectives, per_device(): lax.all_gather(keys, 'half', axis=0, tiled=True)  7.24 us
    all_gather x1, blocking collectives, per_device(): lax.all_gather(values, 'half', axis=0, tiled=True)  7.21 us
    dot_general x1, matrix products, attend(): jnp.einsum('qhd,khd->hqk', q3, k3, preferred_element_type=jnp.float32)  6.24 us
    another operation x3, local copies, waits for them, and re-layouts  5.44 us
    dot_general x1, matrix products, attend(): jnp.einsum('hqk,khd->qhd', weights.astype(jnp.bfloat16), v3, preferred_el...  5.18 us
    reduce_sum x1, other arithmetic, attend(): total = jnp.sum(weights, axis=2)  3.21 us
  transfers between devices with their start and end apart: 2, of which 2 were waited for; matrix products, arithmetic and copies ran while one was open for 2% of the time, Pallas kernels for 0%

commit v1 on v0

v1 whole, which is shorter than its diff:
```python
import functools

import jax
import jax.numpy as jnp
from jax import lax
from jax.experimental import pallas as pl
from jax.experimental.pallas import tpu as pltpu
from jax.sharding import PartitionSpec as P

HEADS = 4
NEG = -1e30
MESH = pl.DeviceIdType.MESH


def body(
    sizes,
    lists_ref,
    lens_ref,
    tokens_ref,
    w_ref,
    w_out_ref,
    out_ref,
    x,
    w,
    wo,
    kbuf,
    vbuf,
    weight_buf,
    total_buf,
    load_sem,
    send_sem,
    recv_sem,
):
    views, halves = sizes
    view, half = lax.axis_index("view"), lax.axis_index("half")
    count, block, inner = kbuf.shape
    local = count // (views * halves)
    rows = local * block
    head_size = inner // HEADS
    slots = lists_ref.shape[1]
    bufs = (kbuf, vbuf)

    loads = [pltpu.make_async_copy(tokens_ref, x, load_sem.at[0])]
    for n, group in enumerate((1, 2, 0)):
        cols = pl.ds(group * inner, inner)
        loads.append(
            pltpu.make_async_copy(w_ref.at[:, cols], w.at[group], load_sem.at[1 + n])
        )
    loads.append(pltpu.make_async_copy(w_out_ref, wo, load_sem.at[4]))
    for load in loads:
        load.start()

    toward = (
        (view + 1 < views, {"view": view + 1}, views),
        (view >= 1, {"view": view - 1}, views),
        (half + 1 < halves, {"half": half + 1}, halves),
        (half >= 1, {"half": half - 1}, halves),
    )

    barrier = pltpu.get_barrier_semaphore()
    for there, device, size in toward:
        if size > 1:

            @pl.when(there)
            def _():
                pl.semaphore_signal(barrier, inc=1, device_id=device, device_id_type=MESH)

    def piece(c, slot, way):
        rows_of = bufs[c].at[pl.ds(slot * local, local)]
        return pltpu.make_async_remote_copy(
            src_ref=rows_of,
            dst_ref=rows_of,
            send_sem=send_sem.at[way, c, slot],
            recv_sem=recv_sem.at[c, slot],
            device_id=toward[way][1],
            device_id_type=MESH,
        )

    sends = []

    def send(c, slot, way, here):
        there, _, size = toward[way]
        if size == 1:
            return
        cond = there if here is None else jnp.logical_and(here, there)
        sends.append((cond, c, slot, way))

        @pl.when(cond)
        def _():
            piece(c, slot, way).start()

    def arrive(c, slot, here):
        @pl.when(here)
        def _():
            piece(c, slot, 0).wait_recv()

    def project(group):
        return jnp.dot(x[...], w[group], preferred_element_type=jnp.float32).astype(
            jnp.bfloat16
        )

    own = view * halves + half
    loads[0].wait()
    for c in range(2):
        loads[1 + c].wait()
        bufs[c][pl.ds(own * local, local)] = project(1 + c).reshape(local, block, inner)
        if c == 0:
            expected = sum(there.astype(jnp.int32) for there, _, size in toward if size > 1)
            pl.semaphore_wait(barrier, expected)
        for way in (2, 3, 0, 1):
            send(c, own, way, None)

    loads[3].wait()
    queries = project(0)
    head_of = lax.broadcasted_iota(jnp.int32, (block, inner), 1) // head_size
    mine = [head_of == h for h in range(HEADS)]

    def along_view(c, dist):
        for sign, way in ((-1, 0), (1, 1)):
            shard = view + sign * dist
            here = shard >= 0 if sign < 0 else shard < views
            slot = shard * halves + half
            arrive(c, slot, here)
            for out in (2, 3):
                send(c, slot, out, here)
            if dist + 1 < views:
                send(c, slot, way, here)

    def along_half(c):
        for far in range(1, halves):
            for dist in range(views):
                for sign in (-1, 1) if dist else (1,):
                    shard = view + sign * dist
                    seen = shard >= 0 if sign < 0 else shard < views
                    for side, way in ((-1, 2), (1, 3)):
                        other = half + side * far
                        here = jnp.logical_and(seen, other >= 0 if side < 0 else other < halves)
                        slot = shard * halves + other
                        arrive(c, slot, here)
                        if far + 1 < halves:
                            send(c, slot, way, here)

    order = [(c, 1) for c in range(2)]
    order += [(c, dist) for c in range(2) for dist in range(2, views)]
    for c, dist in order:
        if dist < views:
            along_view(c, dist)

    along_half(0)
    for i in range(local):
        q = queries[i * block : (i + 1) * block]
        stacked = jnp.concatenate([jnp.where(m, q, jnp.zeros_like(q)) for m in mine], axis=0)
        keys = jnp.concatenate([kbuf[lists_ref[i, s]] for s in range(slots)], axis=0)
        scores = lax.dot_general(
            stacked, keys, (((1,), (1,)), ((), ())), preferred_element_type=jnp.float32
        ) * head_size ** (-0.5)
        live = lax.broadcasted_iota(jnp.int32, scores.shape, 1) // block < lens_ref[i]
        top = jnp.max(jnp.where(live, scores, NEG), axis=1, keepdims=True)
        weights = jnp.where(live, jnp.exp(scores - top), 0.0)
        total_buf[i] = jnp.sum(weights, axis=1, keepdims=True)
        weight_buf[i] = weights.astype(jnp.bfloat16)

    along_half(1)
    loads[4].wait()
    for i in range(local):
        values = jnp.concatenate([vbuf[lists_ref[i, s]] for s in range(slots)], axis=0)
        summed = jnp.dot(weight_buf[i], values, preferred_element_type=jnp.float32)
        scaled = summed / total_buf[i]
        attn = jnp.zeros((block, inner), jnp.float32)
        for h, m in enumerate(mine):
            attn = jnp.where(m, scaled[h * block : (h + 1) * block], attn)
        out_ref[i * block : (i + 1) * block] = jnp.dot(
            attn.astype(jnp.bfloat16), wo[...], preferred_element_type=jnp.float32
        ).astype(out_ref.dtype)

    for cond, c, slot, way in sends:

        @pl.when(cond)
        def _():
            piece(c, slot, way).wait_send()


def per_device(sizes, tokens, w_qkv, w_out, key_lists, list_len):
    views, halves = sizes
    rows, width = tokens.shape[1:]
    inner = w_out.shape[0]
    local = key_lists.shape[1]
    slots = key_lists.shape[2]
    block = rows // local
    shards = views * halves
    anywhere = pl.BlockSpec(memory_space=pl.ANY)
    mixed = pl.pallas_call(
        functools.partial(body, sizes),
        out_shape=jax.ShapeDtypeStruct((rows, width), jnp.bfloat16),
        in_specs=[
            pl.BlockSpec(memory_space=pltpu.SMEM),
            pl.BlockSpec(memory_space=pltpu.SMEM),
            anywhere,
            anywhere,
            anywhere,
        ],
        out_specs=pl.BlockSpec(memory_space=pltpu.VMEM),
        scratch_shapes=[
            pltpu.VMEM((rows, width), jnp.bfloat16),
            pltpu.VMEM((3, width, inner), jnp.bfloat16),
            pltpu.VMEM((inner, width), jnp.bfloat16),
            pltpu.VMEM((shards * local, block, inner), jnp.bfloat16),
            pltpu.VMEM((shards * local, block, inner), jnp.bfloat16),
            pltpu.VMEM((local, HEADS * block, slots * block), jnp.bfloat16),
            pltpu.VMEM((local, HEADS * block, 1), jnp.float32),
            pltpu.SemaphoreType.DMA((5,)),
            pltpu.SemaphoreType.DMA((4, 2, shards)),
            pltpu.SemaphoreType.DMA((2, shards)),
        ],
        compiler_params=pltpu.CompilerParams(collective_id=0, has_side_effects=True),
    )(
        key_lists.reshape(local, slots),
        list_len.reshape(local),
        tokens.reshape(rows, width),
        w_qkv,
        w_out,
    )
    return mixed.reshape(1, rows, width)


def solution(mesh):
    sizes = (mesh.shape["view"], mesh.shape["half"])
    placed = (
        P(("scene", "view"), "half", None),
        P(),
        P(),
        P(("scene", "view"), "half", None),
        P(("scene", "view"), "half"),
    )
    return jax.shard_map(
        functools.partial(per_device, sizes),
        mesh=mesh,
        in_specs=placed,
        out_specs=P(("scene", "view"), "half", None),
        check_vma=False,
    )
```

time: 110 us -> 35.5 us (0.32)
  waiting for transfers between devices: 47.9 us -> 0 us
  Pallas kernels: 0 us -> 33 us
  matrix products: 16.3 us -> 0 us
  blocking collectives: 14.4 us -> 0 us
  between operations: 14.1 us -> 0.01 us
  local copies, waits for them, and re-layouts: 11.1 us -> 2.3 us
  other arithmetic: 5.97 us -> 0 us
    all_gather x2 -> x0, waiting for transfers between devices: 47.9 us -> none  [the longest x1 28.9 us: per_device(): lax.all_gather(view_values, 'view', axis=0, tiled=True)]
    pallas_call x0 -> x1, Pallas kernels: none -> 33 us  [per_device(): pl.pallas_call(functools.partial(body, sizes), out_shape=jax.ShapeDtypeSt...]
    dot_general x4 -> x0, matrix products: 16.3 us -> none  [the longest x1 6.24 us: attend(): jnp.einsum('qhd,khd->hqk', q3, k3, preferred_element_type=jnp.float32)]
    all_gather x2 -> x0, blocking collectives: 14.4 us -> none  [the longest x1 7.24 us: per_device(): lax.all_gather(keys, 'half', axis=0, tiled=True)]
    another operation x3 -> x0, local copies, waits for them, and re-layouts: 5.44 us -> none
    reduce_sum x1 -> x0, other arithmetic: 3.21 us -> none  [attend(): total = jnp.sum(weights, axis=2)]
    reduce_or x2 -> x0, other arithmetic: 1.98 us -> none  [the longest x1 1.17 us: visit(): jnp.any(allowed)]
    slice x2 -> x0, local copies, waits for them, and re-layouts: 1.59 us -> none  [the longest x1 0.91 us: per_device(): queries = proj[:, :inner]]
  transfers between devices with their start and end apart: 2 -> 0, of which waited for: 2 -> 0; matrix products, arithmetic and copies ran while one was open for 2% -> 0% of each run, Pallas kernels for 0% -> 0%
where the time goes in v1:
time: 35.5 us; the launch traced here: 35.3 us
  Pallas kernels  33 us (93%)
  local copies, waits for them, and re-layouts  2.3 us (6%)
    pallas_call x1, Pallas kernels, per_device(): pl.pallas_call(functools.partial(body, sizes), out_shape=jax.ShapeDtypeSt...  33 us
    unnamed x1, local copies, waits for them, and re-layouts  2.3 us

profile of v1, /device:TPU:0, one launch (start us, length us, event | category | flops | bytes accessed | tf_op | source)
XLA Modules:
  0.0 35.3 jit_solution(9311253949565169989)
XLA Ops:
  0.0 33.0 %shard_map.55 = bf16[256,2048]{1,0:T(8,128)(2,1)} custom-call(s32[2,2]{1,0:T(2,128)} %bitcast.6, s32[2]{0:T(128)} %bitcast.7, bf16[256,2048]{1,0:T(8,128)(2,1)} %bitcast.5, bf16[2048,768]{1,0:T(8,128)(2,1)} %w_ref.1, bf16[256,2048]{1,0:T(8,128)(2,1)} %w_out_ref.1), custom_call_target="tpu_custom_call" | custom-call | tf_op jit(solution)/shard_map/pallas_call | solution.py:192
  33.0 2.3 %copy.7 = bf16[1,256,2048]{2,1,0:T(8,128)(2,1)} copy(bf16[1,256,2048]{2,1,0:T(8,128)(2,1)} %bitcast.4) | data formatting | bytes 2097152

commit v2 on v1

--- a/solution.py
+++ b/solution.py
@@ -18,11 +18,9 @@
     lens_ref,
     tokens_ref,
     w_ref,
-    w_out_ref,
     out_ref,
     x,
     w,
-    wo,
     kbuf,
     vbuf,
     weight_buf,
@@ -46,7 +44,6 @@
         loads.append(
             pltpu.make_async_copy(w_ref.at[:, cols], w.at[group], load_sem.at[1 + n])
         )
-    loads.append(pltpu.make_async_copy(w_out_ref, wo, load_sem.at[4]))
     for load in loads:
         load.start()
 
@@ -161,7 +158,6 @@
         weight_buf[i] = weights.astype(jnp.bfloat16)
 
     along_half(1)
-    loads[4].wait()
     for i in range(local):
         values = jnp.concatenate([vbuf[lists_ref[i, s]] for s in range(slots)], axis=0)
         summed = jnp.dot(weight_buf[i], values, preferred_element_type=jnp.float32)
@@ -169,9 +165,7 @@
         attn = jnp.zeros((block, inner), jnp.float32)
         for h, m in enumerate(mine):
             attn = jnp.where(m, scaled[h * block : (h + 1) * block], attn)
-        out_ref[i * block : (i + 1) * block] = jnp.dot(
-            attn.astype(jnp.bfloat16), wo[...], preferred_element_type=jnp.float32
-        ).astype(out_ref.dtype)
+        out_ref[i * block : (i + 1) * block] = attn.astype(out_ref.dtype)
 
     for cond, c, slot, way in sends:
 
@@ -189,13 +183,12 @@
     block = rows // local
     shards = views * halves
     anywhere = pl.BlockSpec(memory_space=pl.ANY)
-    mixed = pl.pallas_call(
+    attn = pl.pallas_call(
         functools.partial(body, sizes),
-        out_shape=jax.ShapeDtypeStruct((rows, width), jnp.bfloat16),
+        out_shape=jax.ShapeDtypeStruct((rows, inner), jnp.bfloat16),
         in_specs=[
             pl.BlockSpec(memory_space=pltpu.SMEM),
             pl.BlockSpec(memory_space=pltpu.SMEM),
-            anywhere,
             anywhere,
             anywhere,
         ],
@@ -203,12 +196,11 @@
         scratch_shapes=[
             pltpu.VMEM((rows, width), jnp.bfloat16),
             pltpu.VMEM((3, width, inner), jnp.bfloat16),
-            pltpu.VMEM((inner, width), jnp.bfloat16),
             pltpu.VMEM((shards * local, block, inner), jnp.bfloat16),
             pltpu.VMEM((shards * local, block, inner), jnp.bfloat16),
             pltpu.VMEM((local, HEADS * block, slots * block), jnp.bfloat16),
             pltpu.VMEM((local, HEADS * block, 1), jnp.float32),
-            pltpu.SemaphoreType.DMA((5,)),
+            pltpu.SemaphoreType.DMA((4,)),
             pltpu.SemaphoreType.DMA((4, 2, shards)),
             pltpu.SemaphoreType.DMA((2, shards)),
         ],
@@ -218,8 +210,8 @@
         list_len.reshape(local),
         tokens.reshape(rows, width),
         w_qkv,
-        w_out,
-    )
+    )
+    mixed = jnp.dot(attn, w_out, preferred_element_type=jnp.float32).astype(jnp.bfloat16)
     return mixed.reshape(1, rows, width)
 
 

time: 35.5 us -> 34.8 us (0.980)
  matrix products: 0 us -> 2.32 us
  local copies, waits for them, and re-layouts: 2.3 us -> 0.01 us
  Pallas kernels: 33 us -> 32.3 us
    dot_general x0 -> x1, matrix products: none -> 2.32 us  [per_device(): jnp.dot(attn, w_out, preferred_element_type=jnp.float32)]
    unnamed x1 -> x2, local copies, waits for them, and re-layouts: 2.3 us -> 0.01 us
    pallas_call x1, Pallas kernels: 33 us -> 32.3 us  [per_device(): pl.pallas_call(functools.partial(body, sizes), out_shape=jax.ShapeDtypeSt...]
where the time goes in v2:
time: 34.8 us; the launch traced here: 34.6 us
  Pallas kernels  32.3 us (93%)
  matrix products  2.32 us (7%)
    pallas_call x1, Pallas kernels, per_device(): pl.pallas_call(functools.partial(body, sizes), out_shape=jax.ShapeDtypeSt...  32.3 us
    dot_general x1, matrix products, per_device(): jnp.dot(attn, w_out, preferred_element_type=jnp.float32)  2.32 us

profile of v2, /device:TPU:0, one launch (start us, length us, event | category | flops | bytes accessed | tf_op | source)
XLA Modules:
  0.0 34.6 jit_solution(5989579739652292985)
XLA Ops:
  0.0 0.0 copy-start
  0.0 32.3 %shard_map.55 = bf16[256,256]{1,0:T(8,128)(2,1)} custom-call(s32[2,2]{1,0:T(2,128)} %bitcast.8, s32[2]{0:T(128)} %bitcast.9, bf16[256,2048]{1,0:T(8,128)(2,1)} %bitcast.7, bf16[2048,768]{1,0:T(8,128)(2,1)} %w_ref.1), custom_call_target="tpu_custom_call" | custom-call | tf_op jit(solution)/shard_map/pallas_call | solution.py:186
  32.3 0.0 copy-done
  32.3 2.3 %fusion = bf16[1,256,2048]{2,1,0:T(8,128)(2,1)} fusion(bf16[256,256]{1,0:T(8,128)(2,1)} %shard_map.55, bf16[256,2048]{1,0:T(8,128)(2,1)S(1)} %copy-done), kind=kOutput, calls=%fused_computation.1 | convolution fusion | flops 268959744 | bytes 2228224 | tf_op jit(solution)/shard_map/dot_general | solution.py:214
Async XLA Ops:
  0.0 32.3 %copy-start = (bf16[256,2048]{1,0:T(8,128)(2,1)S(1)}, bf16[256,2048]{1,0:T(8,128)(2,1)}, u32[]{:S(2)}) copy-start(bf16[256,2048]{1,0:T(8,128)(2,1)} %param.7) | copy-start | bytes 3145732

commit v3 on v2

--- a/solution.py
+++ b/solution.py
@@ -63,7 +63,7 @@
                 pl.semaphore_signal(barrier, inc=1, device_id=device, device_id_type=MESH)
 
     def piece(c, slot, way):
-        rows_of = bufs[c].at[pl.ds(slot * local, local)]
+        rows_of = bufs[c].at[slot]
         return pltpu.make_async_remote_copy(
             src_ref=rows_of,
             dst_ref=rows_of,
@@ -104,44 +104,59 @@
         if c == 0:
             expected = sum(there.astype(jnp.int32) for there, _, size in toward if size > 1)
             pl.semaphore_wait(barrier, expected)
-        for way in (2, 3, 0, 1):
-            send(c, own, way, None)
+        for b in range(local):
+            for way in (2, 3, 0, 1):
+                send(c, own * local + b, way, None)
 
     loads[3].wait()
     queries = project(0)
     head_of = lax.broadcasted_iota(jnp.int32, (block, inner), 1) // head_size
     mine = [head_of == h for h in range(HEADS)]
 
+    balanced = halves == 2 and views > 2
+
     def along_view(c, dist):
-        for sign, way in ((-1, 0), (1, 1)):
-            shard = view + sign * dist
-            here = shard >= 0 if sign < 0 else shard < views
-            slot = shard * halves + half
-            arrive(c, slot, here)
-            for out in (2, 3):
-                send(c, slot, out, here)
-            if dist + 1 < views:
-                send(c, slot, way, here)
+        for b in range(local):
+            for sign, way in ((-1, 0), (1, 1)):
+                shard = view + sign * dist
+                here = shard >= 0 if sign < 0 else shard < views
+                slot = (shard * halves + half) * local + b
+                arrive(c, slot, here)
+                across = here
+                if balanced and c == 1 and dist == 1:
+                    across = jnp.logical_and(here, view >= 1) if sign > 0 else None
+                if across is not None:
+                    for out in (2, 3):
+                        send(c, slot, out, across)
+                if dist + 1 < views:
+                    send(c, slot, way, here)
 
     def along_half(c):
         for far in range(1, halves):
-            for dist in range(views):
-                for sign in (-1, 1) if dist else (1,):
-                    shard = view + sign * dist
-                    seen = shard >= 0 if sign < 0 else shard < views
-                    for side, way in ((-1, 2), (1, 3)):
-                        other = half + side * far
-                        here = jnp.logical_and(seen, other >= 0 if side < 0 else other < halves)
-                        slot = shard * halves + other
-                        arrive(c, slot, here)
-                        if far + 1 < halves:
-                            send(c, slot, way, here)
-
-    order = [(c, 1) for c in range(2)]
-    order += [(c, dist) for c in range(2) for dist in range(2, views)]
+            for dist in range(1 if balanced and c == 1 else 0, views):
+                for b in range(local):
+                    for sign in (-1, 1) if dist else (1,):
+                        shard = view + sign * dist
+                        seen = shard >= 0 if sign < 0 else shard < views
+                        for side, way in ((-1, 2), (1, 3)):
+                            other = half + side * far
+                            here = jnp.logical_and(
+                                seen, other >= 0 if side < 0 else other < halves
+                            )
+                            slot = (shard * halves + other) * local + b
+                            arrive(c, slot, here)
+                            if far + 1 < halves:
+                                send(c, slot, way, here)
+
+    order = [(c, dist) for dist in range(1, views) for c in range(2)]
     for c, dist in order:
-        if dist < views:
-            along_view(c, dist)
+        along_view(c, dist)
+    if balanced:
+        for b in range(local):
+            slot = (view * halves + (halves - 1) - half) * local + b
+            arrive(1, slot, view >= 0)
+            send(1, slot, 0, None)
+            send(1, slot, 1, view == 1)
 
     along_half(0)
     for i in range(local):
@@ -201,8 +216,8 @@
             pltpu.VMEM((local, HEADS * block, slots * block), jnp.bfloat16),
             pltpu.VMEM((local, HEADS * block, 1), jnp.float32),
             pltpu.SemaphoreType.DMA((4,)),
-            pltpu.SemaphoreType.DMA((4, 2, shards)),
-            pltpu.SemaphoreType.DMA((2, shards)),
+            pltpu.SemaphoreType.DMA((4, 2, shards * local)),
+            pltpu.SemaphoreType.DMA((2, shards * local)),
         ],
         compiler_params=pltpu.CompilerParams(collective_id=0, has_side_effects=True),
     )(

time: 34.8 us -> 33.4 us (0.960)
  Pallas kernels: 32.3 us -> 30.9 us
    pallas_call x1, Pallas kernels: 32.3 us -> 30.9 us  [per_device(): pl.pallas_call(functools.partial(body, sizes), out_shape=jax.ShapeDtypeSt...]
where the time goes in v3:
time: 33.4 us; the launch traced here: 33.3 us
  Pallas kernels  30.9 us (93%)
  matrix products  2.32 us (7%)
    pallas_call x1, Pallas kernels, per_device(): pl.pallas_call(functools.partial(body, sizes), out_shape=jax.ShapeDtypeSt...  30.9 us
    dot_general x1, matrix products, per_device(): jnp.dot(attn, w_out, preferred_element_type=jnp.float32)  2.32 us

profile of v3, /device:TPU:0, one launch (start us, length us, event | category | flops | bytes accessed | tf_op | source)
XLA Modules:
  0.0 33.3 jit_solution(2307992512642917342)
XLA Ops:
  0.0 0.0 copy-start
  0.0 30.9 %shard_map.55 = bf16[256,256]{1,0:T(8,128)(2,1)} custom-call(s32[2,2]{1,0:T(2,128)} %bitcast.8, s32[2]{0:T(128)} %bitcast.9, bf16[256,2048]{1,0:T(8,128)(2,1)} %bitcast.7, bf16[2048,768]{1,0:T(8,128)(2,1)} %w_ref.1), custom_call_target="tpu_custom_call" | custom-call | tf_op jit(solution)/shard_map/pallas_call | solution.py:201
  31.0 0.0 copy-done
  31.0 2.3 %fusion = bf16[1,256,2048]{2,1,0:T(8,128)(2,1)} fusion(bf16[256,256]{1,0:T(8,128)(2,1)} %shard_map.55, bf16[256,2048]{1,0:T(8,128)(2,1)S(1)} %copy-done), kind=kOutput, calls=%fused_computation.1 | convolution fusion | flops 268959744 | bytes 2228224 | tf_op jit(solution)/shard_map/dot_general | solution.py:229
Async XLA Ops:
  0.0 31.0 %copy-start = (bf16[256,2048]{1,0:T(8,128)(2,1)S(1)}, bf16[256,2048]{1,0:T(8,128)(2,1)}, u32[]{:S(2)}) copy-start(bf16[256,2048]{1,0:T(8,128)(2,1)} %param.7) | copy-start | bytes 3145732

commit v4 on v3

--- a/solution.py
+++ b/solution.py
@@ -114,6 +114,7 @@
     mine = [head_of == h for h in range(HEADS)]
 
     balanced = halves == 2 and views > 2
+    last = views - 1
 
     def along_view(c, dist):
         for b in range(local):
@@ -123,21 +124,30 @@
                 slot = (shard * halves + half) * local + b
                 arrive(c, slot, here)
                 across = here
-                if balanced and c == 1 and dist == 1:
-                    across = jnp.logical_and(here, view >= 1) if sign > 0 else None
-                if across is not None:
-                    for out in (2, 3):
-                        send(c, slot, out, across)
+                if balanced and c == 1:
+                    across = shard >= 1 if sign < 0 else shard < last
+                for out in (2, 3):
+                    send(c, slot, out, across)
                 if dist + 1 < views:
                     send(c, slot, way, here)
 
+    def relay(dist):
+        for b in range(local):
+            for shard, here, way in ((0, view == dist, 0), (last, view == last - dist, 1)):
+                slot = (shard * halves + (halves - 1) - half) * local + b
+                arrive(1, slot, here)
+                if dist < last:
+                    send(1, slot, way, here)
+
     def along_half(c):
         for far in range(1, halves):
-            for dist in range(1 if balanced and c == 1 else 0, views):
+            for dist in range(views):
                 for b in range(local):
                     for sign in (-1, 1) if dist else (1,):
                         shard = view + sign * dist
                         seen = shard >= 0 if sign < 0 else shard < views
+                        if balanced and c == 1:
+                            seen = jnp.logical_and(shard >= 1, shard < last)
                         for side, way in ((-1, 2), (1, 3)):
                             other = half + side * far
                             here = jnp.logical_and(
@@ -148,15 +158,13 @@
                             if far + 1 < halves:
                                 send(c, slot, way, here)
 
-    order = [(c, dist) for dist in range(1, views) for c in range(2)]
-    for c, dist in order:
-        along_view(c, dist)
-    if balanced:
-        for b in range(local):
-            slot = (view * halves + (halves - 1) - half) * local + b
-            arrive(1, slot, view >= 0)
-            send(1, slot, 0, None)
-            send(1, slot, 1, view == 1)
+    for dist in range(1, views):
+        along_view(0, dist)
+        if balanced and dist > 1:
+            relay(dist - 1)
+        along_view(1, dist)
+        if balanced and dist == 1:
+            relay(0)
 
     along_half(0)
     for i in range(local):
@@ -173,6 +181,8 @@
         weight_buf[i] = weights.astype(jnp.bfloat16)
 
     along_half(1)
+    if balanced:
+        relay(last)
     for i in range(local):
         values = jnp.concatenate([vbuf[lists_ref[i, s]] for s in range(slots)], axis=0)
         summed = jnp.dot(weight_buf[i], values, preferred_element_type=jnp.float32)

time: 33.4 us -> 32.3 us (0.967)
  Pallas kernels: 30.9 us -> 29.8 us
    pallas_call x1, Pallas kernels: 30.9 us -> 29.8 us  [per_device(): pl.pallas_call(functools.partial(body, sizes), out_shape=jax.ShapeDtypeSt...]
where the time goes in v4:
time: 32.3 us; the launch traced here: 32.1 us
  Pallas kernels  29.8 us (92%)
  matrix products  2.32 us (7%)
    pallas_call x1, Pallas kernels, per_device(): pl.pallas_call(functools.partial(body, sizes), out_shape=jax.ShapeDtypeSt...  29.8 us
    dot_general x1, matrix products, per_device(): jnp.dot(attn, w_out, preferred_element_type=jnp.float32)  2.32 us

profile of v4, /device:TPU:0, one launch (start us, length us, event | category | flops | bytes accessed | tf_op | source)
XLA Modules:
  0.0 32.1 jit_solution(17832173679028742168)
XLA Ops:
  0.0 0.0 copy-start
  0.0 29.8 %shard_map.55 = bf16[256,256]{1,0:T(8,128)(2,1)} custom-call(s32[2,2]{1,0:T(2,128)} %bitcast.8, s32[2]{0:T(128)} %bitcast.9, bf16[256,2048]{1,0:T(8,128)(2,1)} %bitcast.7, bf16[2048,768]{1,0:T(8,128)(2,1)} %w_ref.1), custom_call_target="tpu_custom_call" | custom-call | tf_op jit(solution)/shard_map/pallas_call | solution.py:211
  29.8 0.0 copy-done
  29.8 2.3 %fusion = bf16[1,256,2048]{2,1,0:T(8,128)(2,1)} fusion(bf16[256,256]{1,0:T(8,128)(2,1)} %shard_map.55, bf16[256,2048]{1,0:T(8,128)(2,1)S(1)} %copy-done), kind=kOutput, calls=%fused_computation.1 | convolution fusion | flops 268959744 | bytes 2228224 | tf_op jit(solution)/shard_map/dot_general | solution.py:239
Async XLA Ops:
  0.0 29.8 %copy-start = (bf16[256,2048]{1,0:T(8,128)(2,1)S(1)}, bf16[256,2048]{1,0:T(8,128)(2,1)}, u32[]{:S(2)}) copy-start(bf16[256,2048]{1,0:T(8,128)(2,1)} %param.7) | copy-start | bytes 3145732

commit v5 on v4

--- a/solution.py
+++ b/solution.py
@@ -44,7 +44,7 @@
         loads.append(
             pltpu.make_async_copy(w_ref.at[:, cols], w.at[group], load_sem.at[1 + n])
         )
-    for load in loads:
+    for load in loads[:2]:
         load.start()
 
     toward = (
@@ -100,11 +100,14 @@
     loads[0].wait()
     for c in range(2):
         loads[1 + c].wait()
-        bufs[c][pl.ds(own * local, local)] = project(1 + c).reshape(local, block, inner)
-        if c == 0:
-            expected = sum(there.astype(jnp.int32) for there, _, size in toward if size > 1)
-            pl.semaphore_wait(barrier, expected)
+        loads[2 + c].start()
         for b in range(local):
+            bufs[c][own * local + b] = jnp.dot(
+                x[b * block : (b + 1) * block], w[1 + c], preferred_element_type=jnp.float32
+            ).astype(jnp.bfloat16)
+            if c == 0 and b == 0:
+                expected = sum(there.astype(jnp.int32) for there, _, size in toward if size > 1)
+                pl.semaphore_wait(barrier, expected)
             for way in (2, 3, 0, 1):
                 send(c, own * local + b, way, None)
 

time: 32.3 us -> 32.1 us (level)
  no operation moved by 1% of the time
where the time goes in v5:
time: 32.1 us; the launch traced here: 31.9 us
  Pallas kernels  29.5 us (92%)
  matrix products  2.32 us (7%)
    pallas_call x1, Pallas kernels, per_device(): pl.pallas_call(functools.partial(body, sizes), out_shape=jax.ShapeDtypeSt...  29.5 us
    dot_general x1, matrix products, per_device(): jnp.dot(attn, w_out, preferred_element_type=jnp.float32)  2.32 us

profile of v5, /device:TPU:0, one launch (start us, length us, event | category | flops | bytes accessed | tf_op | source)
XLA Modules:
  0.0 31.9 jit_solution(5003831197618841135)
XLA Ops:
  0.0 0.0 copy-start
  0.0 29.5 %shard_map.55 = bf16[256,256]{1,0:T(8,128)(2,1)} custom-call(s32[2,2]{1,0:T(2,128)} %bitcast.8, s32[2]{0:T(128)} %bitcast.9, bf16[256,2048]{1,0:T(8,128)(2,1)} %bitcast.7, bf16[2048,768]{1,0:T(8,128)(2,1)} %w_ref.1), custom_call_target="tpu_custom_call" | custom-call | tf_op jit(solution)/shard_map/pallas_call | solution.py:214
  29.6 0.0 copy-done
  29.6 2.3 %fusion = bf16[1,256,2048]{2,1,0:T(8,128)(2,1)} fusion(bf16[256,256]{1,0:T(8,128)(2,1)} %shard_map.55, bf16[256,2048]{1,0:T(8,128)(2,1)S(1)} %copy-done), kind=kOutput, calls=%fused_computation.1 | convolution fusion | flops 268959744 | bytes 2228224 | tf_op jit(solution)/shard_map/dot_general | solution.py:242
Async XLA Ops:
  0.0 29.6 %copy-start = (bf16[256,2048]{1,0:T(8,128)(2,1)S(1)}, bf16[256,2048]{1,0:T(8,128)(2,1)}, u32[]{:S(2)}) copy-start(bf16[256,2048]{1,0:T(8,128)(2,1)} %param.7) | copy-start | bytes 3145732
